TPU v7x, 256 devices: a whole 4x4x8 slice. The times are simulated.
256 devices in a mesh: pipe: 8 (over x, core), bundle: 32 (over z, y).
Axes of the slice: x: 4, y: 4, z: 8, core: 2. Of those that a mesh axis runs over, the one named last changes fastest.
Arguments:
- act_fwd: bfloat16 [8, 2048, 8192], P('pipe', 'bundle'), may hold values from -6 to 6
- grad_in: bfloat16 [8, 2048, 8192], P('pipe', 'bundle'), may hold values from -6 to 6
- w_gate: bfloat16 [8, 8192, 4096], P('pipe', None, 'bundle'), may hold values from -0.0625 to 0.0625
- w_up: bfloat16 [8, 8192, 4096], P('pipe', None, 'bundle'), may hold values from -0.0625 to 0.0625
- w_down: bfloat16 [8, 4096, 8192], P('pipe', 'bundle'), may hold values from -0.09375 to 0.09375
- saved_gate: bfloat16 [8, 2048, 4096], P('pipe', None, 'bundle'), may hold values from -6 to 6
- saved_up: bfloat16 [8, 2048, 4096], P('pipe', None, 'bundle'), may hold values from -6 to 6
- mask_fwd: int32 [8, 128, 32], P('pipe'), may hold values from 0 to 1, as said below
- mask_bwd: int32 [8, 128, 32], P('pipe'), may hold values from 0 to 1, as said below
Outputs:
- next_forward: bfloat16 [8, 2048, 8192], P('pipe', 'bundle')
- next_backward: bfloat16 [8, 2048, 8192], P('pipe', 'bundle')
Inputs may be any that keep to these rules, and one draw needn't show every extreme that they name: `mask_fwd`: within the 4 row blocks of one device's tokens (blocks k * 4 to k * 4 + 3), each bundle is active in at most one. `mask_bwd`: within the 4 row blocks of one device's tokens (blocks k * 4 to k * 4 + 3), each bundle is active in at most one.
All inputs are finite; a program needn't handle non-finite values.
Results may differ from a plain program's by a relative error of at most 0.0033.
Values may be sent and summed in bfloat16 or wider, within the bound.
A program may use at most 128 MiB of HBM per device.

v0:
```python
import jax
import jax.numpy as jnp
from jax import lax
from jax.sharding import PartitionSpec as P

BLOCK = 16


def side_by_side(arrays, axis, split_dim, concat_dim, along):
    ends, at = ([], 0)
    for a in arrays[:-1]:
        at += a.shape[along]
        ends.append(at)
    both = jnp.concatenate(arrays, axis=along)
    return tuple(
        jnp.split(
            lax.all_to_all(both, axis, split_axis=split_dim, concat_axis=concat_dim, tiled=True),
            ends,
            axis=along,
        )
    )


def shifted(value, axis, steps):
    count = lax.axis_size(axis)
    pairs = [(source, (source + steps) % count) for source in range(count)]
    return lax.ppermute(value, axis, pairs)


def contract_last(left, right):
    return lax.dot_general(
        left, right, (((1,), (1,)), ((), ())), preferred_element_type=jnp.float32
    )


def sender_select(mask_all, device, blocks_dev):
    own_rows = lax.dynamic_slice_in_dim(mask_all[0], device * blocks_dev, blocks_dev, 0)
    return own_rows.T.astype(jnp.bfloat16)


def owner_select(mask_all, device, owners, blocks_dev):
    column = lax.dynamic_slice_in_dim(mask_all[0], device, 1, 1)[:, 0]
    return column.reshape(owners, blocks_dev).astype(jnp.bfloat16)


def pack_rows(rows, select, blocks_dev):
    width = rows.shape[-1]
    stacked = rows.reshape(blocks_dev, BLOCK, width)
    packed = jnp.einsum("bj,jtd->btd", select, stacked, preferred_element_type=jnp.float32)
    return packed.astype(jnp.bfloat16)


def pick_saved(saved, select, owners, blocks_dev):
    width = saved.shape[-1]
    stacked = saved.reshape(owners, blocks_dev, BLOCK, width)
    picked = jnp.einsum("kj,kjtu->ktu", select, stacked, preferred_element_type=jnp.float32)
    return picked.astype(jnp.bfloat16).reshape(owners * BLOCK, width)


def place_parts(parts, select, base_rows):
    total = jnp.einsum("bj,btd->jtd", select, parts, preferred_element_type=jnp.float32)
    total = total.reshape(base_rows.shape)
    return (base_rows.astype(jnp.float32) + total).astype(jnp.bfloat16)


def per_device(act_fwd, grad_in, w_gate, w_up, w_down, saved_gate, saved_up, mask_fwd, mask_bwd):
    owners = lax.axis_size("bundle")
    device = lax.axis_index("bundle")
    blocks_dev = act_fwd.shape[1] // BLOCK
    width = act_fwd.shape[2]
    gate_w = w_gate[0]
    up_w = w_up[0]
    down_w = w_down[0]
    select_f = sender_select(mask_fwd, device, blocks_dev)
    select_b = sender_select(mask_bwd, device, blocks_dev)
    packed_f = pack_rows(act_fwd[0], select_f, blocks_dev)
    packed_b = pack_rows(grad_in[0], select_b, blocks_dev)
    owner_b = owner_select(mask_bwd, device, owners, blocks_dev)
    gate_saved = pick_saved(saved_gate[0], owner_b, owners, blocks_dev)
    up_saved = pick_saved(saved_up[0], owner_b, owners, blocks_dev)
    rows_f, rows_b = side_by_side((packed_f, packed_b), "bundle", 0, 0, 1)
    rows = rows_f.reshape(owners * BLOCK, width)
    gate_pre = jnp.dot(rows, gate_w, preferred_element_type=jnp.float32)
    up_pre = jnp.dot(rows, up_w, preferred_element_type=jnp.float32)
    hidden = (jnp.maximum(gate_pre, 0.0) * up_pre).astype(jnp.bfloat16)
    parts_f = (
        jnp.dot(hidden, down_w, preferred_element_type=jnp.float32)
        .astype(jnp.bfloat16)
        .reshape(owners, BLOCK, width)
    )
    grad_hidden = contract_last(rows_b.reshape(owners * BLOCK, width), down_w)
    gate_value = gate_saved.astype(jnp.float32)
    up_value = up_saved.astype(jnp.float32)
    grad_gate = jnp.where(gate_value > 0, grad_hidden * up_value, 0.0).astype(jnp.bfloat16)
    grad_up = (grad_hidden * jnp.maximum(gate_value, 0.0)).astype(jnp.bfloat16)
    summed = contract_last(grad_gate, gate_w) + contract_last(grad_up, up_w)
    parts_b = summed.astype(jnp.bfloat16).reshape(owners, BLOCK, width)
    back_f, back_b = (
        lax.all_to_all(parts_f, "bundle", split_axis=0, concat_axis=0, tiled=True),
        lax.all_to_all(parts_b, "bundle", split_axis=0, concat_axis=0, tiled=True),
    )
    ahead = place_parts(back_f, select_f, act_fwd[0])
    behind = place_parts(back_b, select_b, grad_in[0])
    next_forward = shifted(ahead[None], "pipe", 1)
    next_backward = shifted(behind[None], "pipe", -1)
    return (next_forward, next_backward)


def solution(mesh):
    in_specs = (
        P("pipe", "bundle", None),
        P("pipe", "bundle", None),
        P("pipe", None, "bundle"),
        P("pipe", None, "bundle"),
        P("pipe", "bundle", None),
        P("pipe", None, "bundle"),
        P("pipe", None, "bundle"),
        P("pipe", None, None),
        P("pipe", None, None),
    )
    out_specs = (P("pipe", "bundle", None), P("pipe", "bundle", None))
    return jax.shard_map(
        per_device, mesh=mesh, in_specs=in_specs, out_specs=out_specs, check_vma=False
    )
```

profile of v0, /device:TPU:1, one launch (start us, length us, event | category | flops | bytes accessed | tf_op | source)
XLA Modules:
  0.0 848.0 jit_solution(14979696820518935992)
XLA Ops:
  0.6 0.0 copy-start
  0.6 0.0 copy-start.1
  0.7 1.0 dynamic-slice_convert_fusion
  1.6 0.1 copy.53
  1.7 0.1 copy.52
  1.8 3.6 convolution_convert_fusion.1
  5.5 0.0 copy-done.1
  5.5 2.7 convolution_convert_fusion.2
  8.2 1.6 pad_maximum_fusion
  9.8 22.2 %copy.40 = bf16[32,32,8192]{2,1,0:T(8,128)(2,1)} copy(bf16[32,32,8192]{2,0,1:T(8,128)(2,1)S(1)} %pad_maximum_fusion) | data formatting | bytes 33554432 | tf_op jit(solution)/shard_map/concatenate | solution.py:14
  32.0 375.6 %all_to_all.15 = bf16[32,32,8192]{2,1,0:T(8,128)(2,1)S(1)} all-to-all(bf16[32,32,8192]{2,1,0:T(8,128)(2,1)} %copy.40), channel_id=1, replica_groups=mesh['pipe'=8,'bundle'=32] {'bundle'}, dimensions={0} | all-to-all | bytes 33554432 | tf_op jit(solution)/shard_map/all_to_all | solution.py:17
  407.6 0.0 copy-start.5
  407.6 4.2 fusion.40
  411.8 0.0 copy-start.3
  411.8 0.0 copy-done.5
  411.8 2.3 fusion.10
  414.1 0.0 copy-done.3
  414.1 2.3 fusion.22
  416.4 0.0 copy-done
  416.4 5.6 convolution_convert_fusion
  422.0 7.0 all-to-all-start.1
  429.1 0.7 fusion.39
  429.8 0.1 reshape.53
  429.9 0.0 copy-start.4
  429.9 1.6 fusion.29
  431.6 1.5 fusion.27
  433.1 5.7 fusion.33
  438.8 0.0 copy-done.4
  438.8 0.0 copy-start.6
  438.8 8.1 fusion.12
  446.9 0.0 copy-done.6
  446.9 11.4 %add_convert_fusion = bf16[512,8192]{1,0:T(8,128)(2,1)} fusion(f32[512,8192]{1,0:T(8,128)} %fusion.12, bf16[512,128]{1,0:T(8,128)(2,1)S(1)} %get-tuple-element.4, bf16[1,8192,128]{2,1,0:T(8,128)(2,1)S(1)} %copy-done.6), kind=kOutput, calls=%fused_computation.1 | convolution fusion | flops 1082130432 | bytes 27394048 | tf_op jit(solution)/shard_map/dot_general | solution.py:31
  458.3 160.4 %all-to-all-done.1 = bf16[32,16,8192]{2,1,0:T(8,128)(2,1)} async-done(((bf16[32,16,8192]{2,1,0:T(8,128)(2,1)}), bf16[32,16,8192]{2,1,0:T(8,128)(2,1)}, u32[]{:S(2)}, u32[]{:S(2)}) %all-to-all-start.1) | async-done | bytes 8388640 | tf_op jit(solution)/shard_map/all_to_all | solution.py:99
  618.7 6.2 all-to-all-start.2
  624.9 12.4 %fusion.2 = f32[4,16,8192]{2,0,1:T(4,128)S(1)} fusion(bf16[32,16,8192]{2,1,0:T(8,128)(2,1)} %all-to-all-done.1, bf16[1,4,32]{2,1,0:T(4,128)(2,1)S(1)} %copy.52), kind=kOutput, calls=%fused_computation.7 | convolution fusion | flops 33554432 | bytes 10486016 | tf_op jit(solution)/shard_map/bj,btd->jtd/dot_general | solution.py:61
  637.3 1.2 copy.42
  638.5 1.2 fusion.5
  639.7 0.0 copy-start.2
  639.7 2.9 collective-permute-start
  642.6 172.8 %all-to-all-done.2 = bf16[32,16,8192]{2,1,0:T(8,128)(2,1)} async-done(((bf16[32,16,8192]{2,1,0:T(8,128)(2,1)}), bf16[32,16,8192]{2,1,0:T(8,128)(2,1)}, u32[]{:S(2)}, u32[]{:S(2)}) %all-to-all-start.2) | async-done | bytes 8388640 | tf_op jit(solution)/shard_map/all_to_all | solution.py:100
  815.4 12.6 %fusion = f32[4,16,8192]{2,0,1:T(4,128)S(1)} fusion(bf16[32,16,8192]{2,1,0:T(8,128)(2,1)} %all-to-all-done.2, bf16[1,4,32]{2,1,0:T(4,128)(2,1)S(1)} %copy.53), kind=kOutput, calls=%fused_computation.5 | convolution fusion | flops 33554432 | bytes 10486016 | tf_op jit(solution)/shard_map/bj,btd->jtd/dot_general | solution.py:61
  828.1 1.2 copy.44
  829.3 0.0 copy-done.2
  829.3 0.2 fusion.4
  829.5 1.4 collective-permute-start.1
  831.0 0.0 collective-permute-done
  831.0 13.6 %collective-permute-done.1 = bf16[1,64,8192]{2,1,0:T(8,128)(2,1)S(1)} collective-permute-done((bf16[1,64,8192]{2,1,0:T(8,128)(2,1)S(1)}, bf16[1,64,8192]{2,1,0:T(8,128)(2,1)S(1)}, u32[]{:S(2)}, u32[]{:S(2)}) %collective-permute-start.1) | collective-permute-done | bytes 1048608 | tf_op jit(solution)/shard_map/ppermute | solution.py:27
  844.5 2.3 copy.68
  846.8 1.0 copy.69
  (2 shorter events, 0.1 us)
Async XLA Ops:
  0.6 415.8 %copy-start = (bf16[1,128,8192]{2,1,0:T(8,128)(2,1)S(1)}, bf16[1,128,8192]{2,1,0:T(8,128)(2,1)}, u32[]{:S(2)}) copy-start(bf16[1,128,8192]{2,1,0:T(8,128)(2,1)} %param.13) | copy-start | bytes 6291460
  0.6 4.8 copy-start.1
  407.6 4.2 copy-start.5
  411.8 2.3 copy-start.3
  422.0 196.7 %all-to-all-start.1 = ((bf16[32,16,8192]{2,1,0:T(8,128)(2,1)}), bf16[32,16,8192]{2,1,0:T(8,128)(2,1)}, u32[]{:S(2)}, u32[]{:S(2)}) async-start(bf16[32,16,8192]{2,1,0:T(8,128)(2,1)} %bitcast.74), calls=%async_computation.1 | async-start | bytes 16777216 | tf_op jit(solution)/shard_map/all_to_all | solution.py:99
  429.9 8.9 %copy-start.4 = (bf16[1,8192,128]{2,1,0:T(8,128)(2,1)S(1)}, bf16[1,8192,128]{2,1,0:T(8,128)(2,1)}, u32[]{:S(2)}) copy-start(bf16[1,8192,128]{2,1,0:T(8,128)(2,1)} %param.11) | copy-start | bytes 6291460
  438.8 8.1 copy-start.6
  618.7 196.7 %all-to-all-start.2 = ((bf16[32,16,8192]{2,1,0:T(8,128)(2,1)}), bf16[32,16,8192]{2,1,0:T(8,128)(2,1)}, u32[]{:S(2)}, u32[]{:S(2)}) async-start(bf16[32,16,8192]{2,1,0:T(8,128)(2,1)} %bitcast.75), calls=%async_computation.2 | async-start | bytes 16777216 | tf_op jit(solution)/shard_map/all_to_all | solution.py:100
  639.7 189.6 %copy-start.2 = (bf16[1,64,8192]{2,1,0:T(8,128)(2,1)S(1)}, bf16[1,64,8192]{2,1,0:T(8,128)(2,1)}, u32[]{:S(2)}) copy-start(bf16[1,64,8192]{2,1,0:T(8,128)(2,1)} %param.10) | copy-start | bytes 3145732
  639.7 191.2 %collective-permute-start = (bf16[1,64,8192]{2,1,0:T(8,128)(2,1)}, bf16[1,64,8192]{2,1,0:T(8,128)(2,1)}, u32[]{:S(2)}, u32[]{:S(2)}) collective-permute-start(bf16[1,64,8192]{2,1,0:T(8,128)(2,1)} %fusion.5), channel_id=1, source_target_pairs={{0,32},{32,64},{64,96},{96,128},{128,160},{160,192},{192,224},{224... | collective-permute-start | bytes 3145736 | tf_op jit(solution)/shard_map/ppermute | solution.py:27
  829.5 15.0 %collective-permute-start.1 = (bf16[1,64,8192]{2,1,0:T(8,128)(2,1)S(1)}, bf16[1,64,8192]{2,1,0:T(8,128)(2,1)S(1)}, u32[]{:S(2)}, u32[]{:S(2)}) collective-permute-start(bf16[1,64,8192]{2,1,0:T(8,128)(2,1)S(1)} %fusion.4), channel_id=1, source_target_pairs={{0,224},{32,0},{64,32},{96,64},{128,96},{160,128},{192,160},{224,1... | collective-permute-start | bytes 3145736 | tf_op jit(solution)/shard_map/ppermute | solution.py:27
where the time goes:
time: 854 us; the launch traced here: 848 us
  blocking collectives  376 us (44%)
  waiting for transfers between devices  347 us (41%)
  matrix products  69.9 us (8%)
  local copies, waits for them, and re-layouts  32.4 us (4%)
  starting transfers between devices  17.5 us (2%)
    all_to_all x1, blocking collectives, side_by_side(): lax.all_to_all(both, axis, split_axis=split_dim, concat_axis=concat_dim,...  376 us
    all_to_all x1, waiting for transfers between devices, per_device(): lax.all_to_all(parts_b, 'bundle', split_axis=0, concat_axis=0, tiled=True)  173 us
    all_to_all x1, waiting for transfers between devices, per_device(): lax.all_to_all(parts_f, 'bundle', split_axis=0, concat_axis=0, tiled=True)  160 us
    dot_general x3, matrix products, contract_last(): lax.dot_general(left, right, (((1,), (1,)), ((), ())), preferred_element_...  25.2 us
    dot_general x2, matrix products, place_parts(): jnp.einsum('bj,btd->jtd', select, parts, preferred_element_type=jnp.float32)  25.1 us
    concatenate x1, local copies, waits for them, and re-layouts, side_by_side(): both = jnp.concatenate(arrays, axis=along)  22.2 us
  transfers between devices with their start and end apart: 4, of which 3 were waited for; matrix products, arithmetic and copies ran while one was open for 7% of the time, Pallas kernels for 0%

commit v1 on v0

v1 whole, which is shorter than its diff:
```python
import functools

import jax
import jax.numpy as jnp
from jax import lax
from jax.experimental import pallas as pl
from jax.experimental.pallas import tpu as pltpu
from jax.sharding import PartitionSpec as P

MESH = pl.DeviceIdType.MESH
F32, BF16 = jnp.float32, jnp.bfloat16
NZ, NY = 8, 4
BLOCK = 16
Z_REL = (0, 1, -1, 2, -2, 3, -3, 4)
RIGHT, LEFT = 0, 1
RING = 4
QUARTERS = 4


def slot_of(direction, step):
    if step == 4:
        return 7
    return 2 * step if direction == RIGHT else 2 * step - 1


def aligned(x, n):
    return pl.multiple_of(x, n)


def kernel(
    chunks,
    act_hbm,
    grad_hbm,
    wg_hbm,
    wu_hbm,
    wd_hbm,
    sg_hbm,
    su_hbm,
    mask_f,
    mask_b,
    out_f,
    out_b,
    tok_f,
    tok_b,
    wgu,
    wd,
    sg,
    su,
    hid,
    grads,
    acc,
    part,
    sbuf,
    rbuf,
    obuf,
    local_sem,
    z_send,
    z_recv,
    y_send,
    y_recv,
    s_send,
    s_recv,
    r_send,
    r_recv,
    o_send,
    o_recv,
):
    rows, width = act_hbm.shape
    half = rows // 2
    bw = wg_hbm.shape[1]
    n_pipe = lax.axis_size("pipe")
    pipe = lax.axis_index("pipe")
    k = lax.axis_index("bundle")
    z, y = k // NY, k % NY
    z_next = ((z + 1) % NZ) * NY + y
    z_prev = ((z + NZ - 1) % NZ) * NY + y
    y_next = z * NY + (y + 1) % NY
    y_prev = z * NY + (y + NY - 1) % NY
    y_far = z * NY + (y + 2) % NY
    p_next = (pipe + 1) % n_pipe
    p_prev = (pipe + n_pipe - 1) % n_pipe
    z_to = ((pipe, z_next), (pipe, z_prev))
    y_to = ((pipe, y_next), (pipe, y_prev))
    toks = (tok_f, tok_b)
    toks_hbm = (act_hbm, grad_hbm)
    cols = width // chunks
    qcols = width // QUARTERS
    per_q = chunks // QUARTERS

    def remote(src, dst, send, recv, to):
        return pltpu.make_async_remote_copy(
            src_ref=src,
            dst_ref=dst,
            send_sem=send,
            recv_sem=recv,
            device_id=to,
            device_id_type=MESH,
        )

    def token_copy(mb, d, step):
        tok = toks[mb]
        if step == 1:
            src = toks_hbm[mb]
        elif step == 4:
            src = tok.at[pl.ds(slot_of(d, 3) * rows + d * half, half), :]
        else:
            src = tok.at[pl.ds(slot_of(d, step - 1) * rows, rows), :]
        if step == 4:
            dst = tok.at[pl.ds(7 * rows + d * half, half), :]
        else:
            dst = tok.at[pl.ds(slot_of(d, step) * rows, rows), :]
        return remote(
            src, dst, z_send.at[mb, d, step - 1], z_recv.at[mb, d, step - 1], z_to[d]
        )

    hw = width // 2
    hb = bw // 2

    def weight_copy(d, piece):
        j = 2 if d == RIGHT else 1
        if piece == 0:
            src, dst = wg_hbm, wgu.at[j, :, pl.ds(0, bw)]
        elif piece == 1:
            src, dst = wu_hbm, wgu.at[j, :, pl.ds(bw, bw)]
        elif piece < 4:
            lanes = pl.ds((piece - 2) * bw, bw)
            src = wgu.at[j, pl.ds(d * hw, hw), lanes]
            dst = wgu.at[3, pl.ds(d * hw, hw), lanes]
        elif piece < 8:
            part_cols = pl.ds((piece - 4) * qcols, qcols)
            src = wd_hbm.at[:, part_cols]
            dst = wd.at[pl.ds(j * bw, bw), part_cols]
        else:
            part_cols = pl.ds((piece - 8) * qcols, qcols)
            src = wd.at[pl.ds(j * bw + d * hb, hb), part_cols]
            dst = wd.at[pl.ds(3 * bw + d * hb, hb), part_cols]
        return remote(src, dst, y_send.at[d, piece], y_recv.at[d, piece], y_to[d])

    def saved_copy(peer, which):
        to_y = (y + (1, NY - 1, 2)[peer]) % NY
        to = (pipe, (y_next, y_prev, y_far)[peer])
        j = (2, 1, 3)[peer]
        src = (sg_hbm, su_hbm)[which].at[:, to_y]
        dst = (sg, su)[which].at[j]
        return remote(src, dst, s_send.at[peer, which], s_recv.at[peer, which], to)

    def ring_copy(d, step, c):
        n = half if step == 1 else rows
        r0 = d * half if step == 1 else 0
        b = c % RING
        return remote(
            sbuf.at[d, step - 1, b, pl.ds(r0, n), :],
            rbuf.at[d, step - 1, b, pl.ds(r0, n), :],
            r_send.at[d, step - 1, b],
            r_recv.at[d, step - 1, b],
            z_to[d],
        )

    def out_copy(mb, c):
        at = pl.ds(aligned(c * cols, cols), cols)
        to = (p_next, k) if mb == 0 else (p_prev, k)
        return remote(
            obuf.at[c % RING],
            (out_f, out_b)[mb].at[:, at],
            o_send.at[c % RING],
            o_recv.at[mb, c],
            to,
        )

    local = [
        pltpu.make_async_copy(src, dst, local_sem.at[i])
        for i, (src, dst) in enumerate(
            (
                (wg_hbm, wgu.at[0, :, pl.ds(0, bw)]),
                (wu_hbm, wgu.at[0, :, pl.ds(bw, bw)]),
                (act_hbm, tok_f.at[pl.ds(0, rows), :]),
                (wd_hbm, wd.at[pl.ds(0, bw), :]),
                (grad_hbm, tok_b.at[pl.ds(0, rows), :]),
                (sg_hbm.at[:, y], sg.at[0]),
                (su_hbm.at[:, y], su.at[0]),
            )
        )
    ]

    barrier = pltpu.get_barrier_semaphore()
    for to in z_to + y_to + ((pipe, y_far), (p_next, k), (p_prev, k)):
        pl.semaphore_signal(barrier, inc=1, device_id=to, device_id_type=MESH)
    pl.semaphore_wait(barrier, 7)

    for mb in (0, 1):
        for d in (0, 1):
            token_copy(mb, d, 1).start()
    for piece in (0, 1):
        for d in (0, 1):
            weight_copy(d, piece).start()
    for copy in local:
        copy.start()

    def pass_tokens(mb, step):
        for d in (0, 1):
            token_copy(mb, d, step).wait_recv()
            if step < 4:
                token_copy(mb, d, step + 1).start()

    def pass_weights(piece, onward):
        for d in (0, 1):
            weight_copy(d, piece).wait_recv()
            weight_copy(d, onward).start()

    deep = width // 8

    def hidden_for(j_from, j_to, first_slot, slots):
        r0, m = first_slot * rows, slots * rows

        @pl.loop(j_from, j_to)
        def _(j):
            both = pl.ds(0, 2 * bw)
            acc[pl.ds(0, m), both] = jnp.zeros((m, 2 * bw), F32)

            @pl.loop(0, 8)
            def _(kc):
                at = pl.ds(aligned(kc * deep, deep), deep)
                acc[pl.ds(0, m), both] += jnp.dot(
                    tok_f[pl.ds(r0, m), at], wgu[j, at, :], preferred_element_type=F32
                )

            bundle = z * NY + (y + j + j // 2 - 2 * (j // 3)) % NY
            lanes = pl.ds(aligned(j * bw, bw), bw)
            for i in range(slots):
                owner = (z + NZ + Z_REL[first_slot + i]) % NZ
                for b in range(rows // BLOCK):
                    block = (owner * NY + y) * (rows // BLOCK) + b
                    on = mask_f[block, bundle].astype(F32)
                    a0 = i * rows + b * BLOCK
                    gate = acc[pl.ds(a0, BLOCK), pl.ds(0, bw)]
                    up = acc[pl.ds(a0, BLOCK), pl.ds(bw, bw)]
                    hid[pl.ds(r0 + a0, BLOCK), lanes] = (
                        jnp.maximum(gate, 0.0) * up * on
                    ).astype(BF16)

    pass_tokens(0, 1)
    pass_tokens(1, 1)
    pass_weights(0, 2)
    pass_tokens(0, 2)
    pass_tokens(1, 2)
    pass_weights(1, 3)
    for d in (0, 1):
        weight_copy(d, 4).start()
    pass_tokens(0, 3)
    for copy in local:
        copy.wait()
    hidden_for(0, 3, 0, 7)
    pass_tokens(1, 3)
    for d in (0, 1):
        weight_copy(d, 2).wait_recv()
        weight_copy(d, 3).wait_recv()
    hidden_for(3, 4, 0, 7)
    pass_tokens(0, 4)
    hidden_for(0, 4, 7, 1)
    pass_weights(4, 8)
    for d in (0, 1):
        weight_copy(d, 5).start()

    gh = acc
    n_part = part.shape[0]

    def grads_for():
        for j in range(NY):
            rel = (0, 1, 3, 2)[j]
            bundle = z * NY + (y + rel) % NY
            for i in range(NZ):
                owner = (z + NZ + Z_REL[i]) % NZ
                for b in range(rows // BLOCK):
                    block = (owner * NY + y) * (rows // BLOCK) + b
                    on = mask_b[block, bundle].astype(F32)
                    at = pl.ds(i * rows + b * BLOCK, BLOCK)
                    grad = gh[at, pl.ds(j * bw, bw)] * on
                    in_block = pl.ds(b * BLOCK, BLOCK)
                    gate = sg[j, owner, in_block, :].astype(F32)
                    up = su[j, owner, in_block, :].astype(F32)
                    grads[at, pl.ds(2 * j * bw, bw)] = jnp.where(
                        gate > 0, grad * up, 0.0
                    ).astype(BF16)
                    grads[at, pl.ds((2 * j + 1) * bw, bw)] = (
                        grad * jnp.maximum(gate, 0.0)
                    ).astype(BF16)

    def side_work(t):
        for q in range(1, QUARTERS):

            @pl.when(t == 3 * q - 2)
            def _():
                pass_weights(4 + q, 8 + q)
                if q < QUARTERS - 1:
                    for d in (0, 1):
                        weight_copy(d, 5 + q).start()
                else:
                    for peer in range(3):
                        for which in (0, 1):
                            saved_copy(peer, which).start()

        for q in range(QUARTERS):

            @pl.when(t == per_q * q)
            def _():
                for d in (0, 1):
                    weight_copy(d, 8 + q).wait_recv()

        @pl.when(t == chunks - 8)
        def _():
            for d in (0, 1):
                token_copy(1, d, 4).wait_recv()
            gh[:, :] = jnp.zeros(gh.shape, F32)

        @pl.when((t >= chunks - 8) & (t < chunks))
        def _():
            at = pl.ds(aligned((t - (chunks - 8)) * deep, deep), deep)
            gh[:, :] += lax.dot_general(
                tok_b[:, at],
                wd[:, at],
                (((1,), (1,)), ((), ())),
                preferred_element_type=F32,
            )

        @pl.when(t == chunks - 1)
        def _():
            for peer in range(3):
                for which in (0, 1):
                    saved_copy(peer, which).wait_recv()
            grads_for()

    def local_part(t):
        @pl.when(t < chunks)
        def _():
            at = pl.ds(aligned(t * cols, cols), cols)
            part[t % n_part] = jnp.dot(hid[...], wd[:, at], preferred_element_type=F32)

        @pl.when((t >= chunks) & (t < 2 * chunks))
        def _():
            at = pl.ds(aligned((t - chunks) * cols, cols), cols)
            total = None
            for j in range(NY):
                piece = lax.dot_general(
                    grads[:, pl.ds(2 * j * bw, 2 * bw)],
                    wgu[j, at, :],
                    (((1,), (1,)), ((), ())),
                    preferred_element_type=F32,
                )
                total = piece if total is None else total + piece
            part[t % n_part] = total

    def ring_step(step, c):
        b = c % RING
        pb = c % n_part
        for d in (0, 1):
            if step > 1:
                ring_copy(d, step - 1, c).wait_recv()

            @pl.when(c >= RING)
            def _():
                ring_copy(d, step, c - RING).wait_send()

            slot = 7 if step == 1 else slot_of(1 - d, 5 - step)
            lo, hi = pl.ds(0, half), pl.ds(half, half)
            mine = pl.ds(d * half, half)
            other = pl.ds((1 - d) * half, half)
            if step == 1:
                at = pl.ds(slot * rows + d * half, half)
                sbuf[d, 0, b, mine, :] = part[pb, at, :].astype(BF16)
            elif step == 2:
                at = pl.ds(slot * rows + d * half, half)
                to = pl.ds(slot * rows + (1 - d) * half, half)
                sbuf[d, 1, b, mine, :] = (
                    part[pb, at, :] + rbuf[d, 0, b, mine, :].astype(F32)
                ).astype(BF16)
                sbuf[d, 1, b, other, :] = part[pb, to, :].astype(BF16)
            else:
                at = pl.ds(slot * rows, rows)
                sbuf[d, step - 1, b] = (
                    part[pb, at, :] + rbuf[d, step - 2, b].astype(F32)
                ).astype(BF16)
            ring_copy(d, step, c).start()

    def finish(c):
        b = c % RING
        for d in (0, 1):
            ring_copy(d, 4, c).wait_recv()

        @pl.when(c >= RING)
        def _():
            out_copy(0, 0 * c + (c - RING) % chunks).wait_send()

        arrived = (
            part[c % n_part, pl.ds(0, rows), :]
            + rbuf[0, 3, b].astype(F32)
            + rbuf[1, 3, b].astype(F32)
        )
        for mb in (0, 1):

            @pl.when((c >= mb * chunks) & (c < (mb + 1) * chunks))
            def _():
                cc = c - mb * chunks
                at = pl.ds(aligned(cc * cols, cols), cols)
                base = toks[mb][pl.ds(0, rows), at].astype(F32)
                obuf[b] = (base + arrived).astype(BF16)
                out_copy(mb, cc).start()

    total = 2 * chunks

    @pl.loop(0, total + 4)
    def _(t):
        side_work(t)
        local_part(t)
        for step in range(1, 5):

            @pl.when((t >= step - 1) & (t < total + step - 1))
            def _():
                ring_step(step, t - (step - 1))

        @pl.when(t >= 4)
        def _():
            finish(t - 4)

    @pl.loop(total - RING, total)
    def _(c):
        for d in (0, 1):
            for step in range(1, 5):
                ring_copy(d, step, c).wait_send()
        out_copy(1, c - chunks).wait_send()

    for mb in (0, 1):
        for d in (0, 1):
            for step in range(1, 5):
                token_copy(mb, d, step).wait_send()
    for d in (0, 1):
        for piece in range(12):
            weight_copy(d, piece).wait_send()
    for peer in range(3):
        for which in (0, 1):
            saved_copy(peer, which).wait_send()

    @pl.loop(0, chunks)
    def _(c):
        for mb in (0, 1):
            out_copy(mb, c).wait_recv()


def per_device(act_fwd, grad_in, w_gate, w_up, w_down, saved_gate, saved_up, mask_fwd, mask_bwd):
    rows, width = act_fwd.shape[1:]
    bw = w_gate.shape[2]
    chunks = 16
    cols = width // chunks
    all_rows = NZ * rows
    by_owner = (NZ, NY, rows, bw)
    anywhere = pl.BlockSpec(memory_space=pl.ANY)
    scalars = pl.BlockSpec(memory_space=pltpu.SMEM)
    dma = pltpu.SemaphoreType.DMA
    out = jax.ShapeDtypeStruct((rows, width), BF16)
    ahead, behind = pl.pallas_call(
        functools.partial(kernel, chunks),
        out_shape=(out, out),
        in_specs=[anywhere] * 7 + [scalars] * 2,
        out_specs=(anywhere, anywhere),
        scratch_shapes=[
            pltpu.VMEM((all_rows, width), BF16),
            pltpu.VMEM((all_rows, width), BF16),
            pltpu.VMEM((NY, width, 2 * bw), BF16),
            pltpu.VMEM((NY * bw, width), BF16),
            pltpu.VMEM((NY, NZ, rows, bw), BF16),
            pltpu.VMEM((NY, NZ, rows, bw), BF16),
            pltpu.VMEM((all_rows, NY * bw), BF16),
            pltpu.VMEM((all_rows, 2 * NY * bw), BF16),
            pltpu.VMEM((all_rows, NY * bw), F32),
            pltpu.VMEM((5, all_rows, cols), F32),
            pltpu.VMEM((2, 4, RING, rows, cols), BF16),
            pltpu.VMEM((2, 4, RING, rows, cols), BF16),
            pltpu.VMEM((RING, rows, cols), BF16),
            dma((7,)),
            dma((2, 2, 4)),
            dma((2, 2, 4)),
            dma((2, 12)),
            dma((2, 12)),
            dma((3, 2)),
            dma((3, 2)),
            dma((2, 4, RING)),
            dma((2, 4, RING)),
            dma((RING,)),
            dma((2, chunks)),
        ],
        compiler_params=pltpu.CompilerParams(
            collective_id=0, has_side_effects=True, vmem_limit_bytes=67043328
        ),
    )(
        act_fwd[0],
        grad_in[0],
        w_gate[0],
        w_up[0],
        w_down[0],
        saved_gate[0].reshape(by_owner),
        saved_up[0].reshape(by_owner),
        mask_fwd[0],
        mask_bwd[0],
    )
    return ahead[None], behind[None]


def solution(mesh):
    in_specs = (
        P("pipe", "bundle", None),
        P("pipe", "bundle", None),
        P("pipe", None, "bundle"),
        P("pipe", None, "bundle"),
        P("pipe", "bundle", None),
        P("pipe", None, "bundle"),
        P("pipe", None, "bundle"),
        P("pipe", None, None),
        P("pipe", None, None),
    )
    out_specs = (P("pipe", "bundle", None), P("pipe", "bundle", None))
    return jax.shard_map(
        per_device, mesh=mesh, in_specs=in_specs, out_specs=out_specs, check_vma=False
    )
```

time: 854 us -> 367 us (0.43)
  blocking collectives: 376 us -> 0 us
  Pallas kernels: 0 us -> 360 us
  waiting for transfers between devices: 347 us -> 0 us
  matrix products: 69.9 us -> 0 us
  local copies, waits for them, and re-layouts: 32.4 us -> 6.22 us
  starting transfers between devices: 17.5 us -> 0 us
    all_to_all x1 -> x0, blocking collectives: 376 us -> none  [side_by_side(): lax.all_to_all(both, axis, split_axis=split_dim, concat_axis=concat_dim,...]
    pallas_call x0 -> x1, Pallas kernels: none -> 360 us  [per_device(): pl.pallas_call(functools.partial(kernel, chunks), out_shape=(out, out), i...]
    all_to_all x2 -> x0, waiting for transfers between devices: 333 us -> none  [the longest x1 173 us: per_device(): lax.all_to_all(parts_b, 'bundle', split_axis=0, concat_axis=0, tiled=True)]
    dot_general x12 -> x0, matrix products: 69.9 us -> none  [the longest x3 25.2 us: contract_last(): lax.dot_general(left, right, (((1,), (1,)), ((), ())), preferred_element_...]
    concatenate x1 -> x0, local copies, waits for them, and re-layouts: 22.2 us -> none  [side_by_side(): both = jnp.concatenate(arrays, axis=along)]
    ppermute x2 -> x0, waiting for transfers between devices: 13.6 us -> none  [shifted(): return lax.ppermute(value, axis, pairs)]
    all_to_all x2 -> x0, starting transfers between devices: 13.2 us -> none  [the longest x1 7.03 us: per_device(): lax.all_to_all(parts_f, 'bundle', split_axis=0, concat_axis=0, tiled=True)]
  transfers between devices with their start and end apart: 4 -> 0, of which waited for: 3 -> 0; matrix products, arithmetic and copies ran while one was open for 7% -> 0% of each run, Pallas kernels for 0% -> 0%
where the time goes in v1:
time: 367 us; the launch traced here: 366 us
  Pallas kernels  360 us (98%)
  local copies, waits for them, and re-layouts  6.22 us (2%)
    pallas_call x1, Pallas kernels, per_device(): pl.pallas_call(functools.partial(kernel, chunks), out_shape=(out, out), i...  360 us

profile of v1, /device:TPU:1, one launch (start us, length us, event | category | flops | bytes accessed | tf_op | source)
XLA Modules:
  0.0 366.4 jit_solution(16048849609925326451)
XLA Ops:
  0.6 1.4 copy.11
  2.1 1.4 copy.12
  3.5 359.5 %shard_map.104 = (bf16[64,8192]{1,0:T(8,128)(2,1)}, bf16[64,8192]{1,0:T(8,128)(2,1)}) custom-call(bf16[64,8192]{1,0:T(8,128)(2,1)} %bitcast.14, bf16[64,8192]{1,0:T(8,128)(2,1)} %bitcast.15, bf16[8192,128]{1,0:T(8,128)(2,1)} %bitcast.11, bf16[8192,128]{1,0:T(8,128)(2,1)} %bitcast.12, bf16[128,8192]{1,0:T(8,128)(2,1)} %bitcast.13, ...), custom_call_target="tpu_custom_call" | custom-call | tf_op jit(solution)/shard_map/pallas_call | solution.py:459
  363.1 0.0 copy-start
  363.1 2.4 copy.15
  365.4 0.0 copy-done
  365.4 1.0 copy.16
Async XLA Ops:
  363.1 2.4 copy-start

commit v2 on v1

--- a/solution.py
+++ b/solution.py
@@ -13,7 +13,8 @@
 BLOCK = 16
 Z_REL = (0, 1, -1, 2, -2, 3, -3, 4)
 RIGHT, LEFT = 0, 1
-RING = 4
+RING = 8
+LAG = 4
 QUARTERS = 4
 
 
@@ -97,21 +98,15 @@
             device_id_type=MESH,
         )
 
-    def token_copy(mb, d, step):
+    def token_copy(mb, d, step, h):
         tok = toks[mb]
         if step == 1:
-            src = toks_hbm[mb]
-        elif step == 4:
-            src = tok.at[pl.ds(slot_of(d, 3) * rows + d * half, half), :]
+            src = toks_hbm[mb].at[pl.ds(h * half, half), :]
         else:
-            src = tok.at[pl.ds(slot_of(d, step - 1) * rows, rows), :]
-        if step == 4:
-            dst = tok.at[pl.ds(7 * rows + d * half, half), :]
-        else:
-            dst = tok.at[pl.ds(slot_of(d, step) * rows, rows), :]
-        return remote(
-            src, dst, z_send.at[mb, d, step - 1], z_recv.at[mb, d, step - 1], z_to[d]
-        )
+            src = tok.at[pl.ds(slot_of(d, step - 1) * rows + h * half, half), :]
+        dst = tok.at[pl.ds(slot_of(d, step) * rows + h * half, half), :]
+        at = (mb, d, step - 1, h)
+        return remote(src, dst, z_send.at[at], z_recv.at[at], z_to[d])
 
     hw = width // 2
     hb = bw // 2
@@ -187,20 +182,27 @@
         pl.semaphore_signal(barrier, inc=1, device_id=to, device_id_type=MESH)
     pl.semaphore_wait(barrier, 7)
 
-    for mb in (0, 1):
-        for d in (0, 1):
-            token_copy(mb, d, 1).start()
+    def send_tokens(mb):
+        for h in (0, 1):
+            for d in (0, 1):
+                token_copy(mb, d, 1, h).start()
+
+    send_tokens(0)
     for piece in (0, 1):
         for d in (0, 1):
             weight_copy(d, piece).start()
     for copy in local:
         copy.start()
 
-    def pass_tokens(mb, step):
-        for d in (0, 1):
-            token_copy(mb, d, step).wait_recv()
-            if step < 4:
-                token_copy(mb, d, step + 1).start()
+    def pass_tokens(mb, step, h):
+        for d in (0, 1):
+            token_copy(mb, d, step, h).wait_recv()
+            if step < 3 or h == d:
+                token_copy(mb, d, step + 1, h).start()
+
+    def last_tokens(mb):
+        for d in (0, 1):
+            token_copy(mb, d, 4, d).wait_recv()
 
     def pass_weights(piece, onward):
         for d in (0, 1):
@@ -209,54 +211,57 @@
 
     deep = width // 8
 
-    def hidden_for(j_from, j_to, first_slot, slots):
-        r0, m = first_slot * rows, slots * rows
-
+    def hidden_for(j_from, j_to):
         @pl.loop(j_from, j_to)
         def _(j):
             both = pl.ds(0, 2 * bw)
-            acc[pl.ds(0, m), both] = jnp.zeros((m, 2 * bw), F32)
+            acc[:, both] = jnp.zeros((NZ * rows, 2 * bw), F32)
 
             @pl.loop(0, 8)
             def _(kc):
                 at = pl.ds(aligned(kc * deep, deep), deep)
-                acc[pl.ds(0, m), both] += jnp.dot(
-                    tok_f[pl.ds(r0, m), at], wgu[j, at, :], preferred_element_type=F32
+                acc[:, both] += jnp.dot(
+                    tok_f[:, at], wgu[j, at, :], preferred_element_type=F32
                 )
 
             bundle = z * NY + (y + j + j // 2 - 2 * (j // 3)) % NY
             lanes = pl.ds(aligned(j * bw, bw), bw)
-            for i in range(slots):
-                owner = (z + NZ + Z_REL[first_slot + i]) % NZ
+            for i in range(NZ):
+                owner = (z + NZ + Z_REL[i]) % NZ
                 for b in range(rows // BLOCK):
                     block = (owner * NY + y) * (rows // BLOCK) + b
-                    on = mask_f[block, bundle].astype(F32)
+                    on = mask_f[bundle, block].astype(F32)
                     a0 = i * rows + b * BLOCK
                     gate = acc[pl.ds(a0, BLOCK), pl.ds(0, bw)]
                     up = acc[pl.ds(a0, BLOCK), pl.ds(bw, bw)]
-                    hid[pl.ds(r0 + a0, BLOCK), lanes] = (
+                    hid[pl.ds(a0, BLOCK), lanes] = (
                         jnp.maximum(gate, 0.0) * up * on
                     ).astype(BF16)
 
-    pass_tokens(0, 1)
-    pass_tokens(1, 1)
+    for step in (1, 2):
+        for h in (0, 1):
+            pass_tokens(0, step, h)
     pass_weights(0, 2)
-    pass_tokens(0, 2)
-    pass_tokens(1, 2)
+    for h in (0, 1):
+        pass_tokens(0, 3, h)
+    send_tokens(1)
+    last_tokens(0)
     pass_weights(1, 3)
     for d in (0, 1):
         weight_copy(d, 4).start()
-    pass_tokens(0, 3)
+    for h in (0, 1):
+        pass_tokens(1, 1, h)
     for copy in local:
         copy.wait()
-    hidden_for(0, 3, 0, 7)
-    pass_tokens(1, 3)
+    hidden_for(0, 3)
+    for h in (0, 1):
+        pass_tokens(1, 2, h)
     for d in (0, 1):
         weight_copy(d, 2).wait_recv()
         weight_copy(d, 3).wait_recv()
-    hidden_for(3, 4, 0, 7)
-    pass_tokens(0, 4)
-    hidden_for(0, 4, 7, 1)
+    hidden_for(3, 4)
+    for h in (0, 1):
+        pass_tokens(1, 3, h)
     pass_weights(4, 8)
     for d in (0, 1):
         weight_copy(d, 5).start()
@@ -272,7 +277,7 @@
                 owner = (z + NZ + Z_REL[i]) % NZ
                 for b in range(rows // BLOCK):
                     block = (owner * NY + y) * (rows // BLOCK) + b
-                    on = mask_b[block, bundle].astype(F32)
+                    on = mask_b[bundle, block].astype(F32)
                     at = pl.ds(i * rows + b * BLOCK, BLOCK)
                     grad = gh[at, pl.ds(j * bw, bw)] * on
                     in_block = pl.ds(b * BLOCK, BLOCK)
@@ -288,7 +293,7 @@
     def side_work(t):
         for q in range(1, QUARTERS):
 
-            @pl.when(t == 3 * q - 2)
+            @pl.when(t == 4 * q - 2)
             def _():
                 pass_weights(4 + q, 8 + q)
                 if q < QUARTERS - 1:
@@ -308,8 +313,7 @@
 
         @pl.when(t == chunks - 8)
         def _():
-            for d in (0, 1):
-                token_copy(1, d, 4).wait_recv()
+            last_tokens(1)
             gh[:, :] = jnp.zeros(gh.shape, F32)
 
         @pl.when((t >= chunks - 8) & (t < chunks))
@@ -388,7 +392,7 @@
 
         @pl.when(c >= RING)
         def _():
-            out_copy(0, 0 * c + (c - RING) % chunks).wait_send()
+            out_copy(0, (c - RING) % chunks).wait_send()
 
         arrived = (
             part[c % n_part, pl.ds(0, rows), :]
@@ -407,19 +411,22 @@
 
     total = 2 * chunks
 
-    @pl.loop(0, total + 4)
+    behind = (0, 1, 2, 3 + LAG, 4 + LAG)
+
+    @pl.loop(0, total + behind[4])
     def _(t):
         side_work(t)
         local_part(t)
         for step in range(1, 5):
-
-            @pl.when((t >= step - 1) & (t < total + step - 1))
+            late = behind[step - 1]
+
+            @pl.when((t >= late) & (t < total + late))
             def _():
-                ring_step(step, t - (step - 1))
-
-        @pl.when(t >= 4)
-        def _():
-            finish(t - 4)
+                ring_step(step, t - late)
+
+        @pl.when(t >= behind[4])
+        def _():
+            finish(t - behind[4])
 
     @pl.loop(total - RING, total)
     def _(c):
@@ -430,8 +437,10 @@
 
     for mb in (0, 1):
         for d in (0, 1):
-            for step in range(1, 5):
-                token_copy(mb, d, step).wait_send()
+            for step in (1, 2, 3):
+                for h in (0, 1):
+                    token_copy(mb, d, step, h).wait_send()
+            token_copy(mb, d, 4, d).wait_send()
     for d in (0, 1):
         for piece in range(12):
             weight_copy(d, piece).wait_send()
@@ -471,13 +480,13 @@
             pltpu.VMEM((all_rows, NY * bw), BF16),
             pltpu.VMEM((all_rows, 2 * NY * bw), BF16),
             pltpu.VMEM((all_rows, NY * bw), F32),
-            pltpu.VMEM((5, all_rows, cols), F32),
+            pltpu.VMEM((5 + LAG, all_rows, cols), F32),
             pltpu.VMEM((2, 4, RING, rows, cols), BF16),
             pltpu.VMEM((2, 4, RING, rows, cols), BF16),
             pltpu.VMEM((RING, rows, cols), BF16),
             dma((7,)),
-            dma((2, 2, 4)),
-            dma((2, 2, 4)),
+            dma((2, 2, 4, 2)),
+            dma((2, 2, 4, 2)),
             dma((2, 12)),
             dma((2, 12)),
             dma((3, 2)),
@@ -498,8 +507,8 @@
         w_down[0],
         saved_gate[0].reshape(by_owner),
         saved_up[0].reshape(by_owner),
-        mask_fwd[0],
-        mask_bwd[0],
+        mask_fwd[0].T,
+        mask_bwd[0].T,
     )
     return ahead[None], behind[None]
 

time: 367 us -> 353 us (0.962)
  Pallas kernels: 360 us -> 348 us
    pallas_call x1, Pallas kernels: 360 us -> 348 us  [per_device(): pl.pallas_call(functools.partial(kernel, chunks), out_shape=(out, out), i...]
where the time goes in v2:
time: 353 us; the launch traced here: 352 us
  Pallas kernels  348 us (99%)
    pallas_call x1, Pallas kernels, per_device(): pl.pallas_call(functools.partial(kernel, chunks), out_shape=(out, out), i...  348 us

profile of v2, /device:TPU:1, one launch (start us, length us, event | category | flops | bytes accessed | tf_op | source)
XLA Modules:
  0.0 352.4 jit_solution(9499161926428316615)
XLA Ops:
  0.6 348.4 %shard_map.104 = (bf16[64,8192]{1,0:T(8,128)(2,1)}, bf16[64,8192]{1,0:T(8,128)(2,1)}) custom-call(bf16[64,8192]{1,0:T(8,128)(2,1)} %bitcast.18, bf16[64,8192]{1,0:T(8,128)(2,1)} %bitcast.19, bf16[8192,128]{1,0:T(8,128)(2,1)} %bitcast.15, bf16[8192,128]{1,0:T(8,128)(2,1)} %bitcast.16, bf16[128,8192]{1,0:T(8,128)(2,1)} %bitcast.17, ...), custom_call_target="tpu_custom_call" | custom-call | tf_op jit(solution)/shard_map/pallas_call | solution.py:468
  349.0 0.0 copy-start
  349.1 2.4 copy.13
  351.4 0.0 copy-done
  351.4 1.0 copy.14
Async XLA Ops:
  349.0 2.4 copy-start

commit v3 on v0

v3 whole, which is shorter than its diff:
```python
import functools

import jax
import jax.numpy as jnp
from jax import lax
from jax.experimental import pallas as pl
from jax.experimental.pallas import tpu as pltpu
from jax.sharding import PartitionSpec as P

MESH = pl.DeviceIdType.MESH
F32, BF16 = jnp.float32, jnp.bfloat16
NZ, NY = 8, 4
BLOCK = 16
Z_REL = (0, 1, -1, 2, -2, 3, -3, 4)
RIGHT, LEFT = 0, 1
RING = 4
QUARTERS = 4
STEPS = 5
FOREIGN = (-1, -2, 1, 2)
FOREIGN_PLACE = (0, 0, 3, 3)


def slot_at(rel):
    rel = (rel + 3) % NZ - 3
    return Z_REL.index(rel)


def aligned(x, n):
    return pl.multiple_of(x, n)


def dot_last(a, b):
    return lax.dot_general(a, b, (((1,), (1,)), ((), ())), preferred_element_type=F32)


def kernel(chunks, *refs):
    (act_hbm, grad_hbm, wg_hbm, wu_hbm, wd_hbm, sg_hbm, su_hbm, mask_f, mask_b) = refs[:9]
    out_f, out_b = refs[9:11]
    (tok_f, tok_b, wgu, wd, sg, su, hid, acc, base_f) = refs[11:20]
    (pk_own, pk_send, pk_recv, hidp, hid_recv) = refs[20:25]
    (ghp, gh_send, gh_recv, gradp, grad_recv) = refs[25:30]
    part, obuf = refs[30:32]
    sbufs, rbufs = refs[32:37], refs[37:42]
    (local_sem, z_send, z_recv, w_send, w_recv, y_send, y_recv, s_send, s_recv) = refs[42:51]
    (x_send, x_recv, r_send, r_recv, o_send, o_recv) = refs[51:57]

    rows, width = act_hbm.shape
    bw = wg_hbm.shape[1]
    pw = width // NZ
    blocks = rows // BLOCK
    n_pipe = lax.axis_size("pipe")
    pipe = lax.axis_index("pipe")
    k = lax.axis_index("bundle")
    z, y = k // NY, k % NY

    def at_z(step):
        return (pipe, ((z + NZ + step) % NZ) * NY + y)

    def at_y(step):
        return (pipe, z * NY + (y + NY + step) % NY)

    p_next = (pipe + 1) % n_pipe
    p_prev = (pipe + n_pipe - 1) % n_pipe
    z_to = (at_z(1), at_z(-1))
    y_to = (at_y(1), at_y(-1))
    toks = (tok_f, tok_b)
    cols = pw // chunks
    qcols = pw // QUARTERS

    def remote(src, dst, send, recv, to):
        return pltpu.make_async_remote_copy(
            src_ref=src,
            dst_ref=dst,
            send_sem=send,
            recv_sem=recv,
            device_id=to,
            device_id_type=MESH,
        )

    def part_of(place):
        return (z + 2 * NZ - place) % NZ

    def part_at(e):
        return pl.ds(aligned(e * pw, pw), pw)

    def token_copy(mb, d, step):
        tok = toks[mb]
        n = (STEPS + 1 - step) * pw
        sign = -1 if d == RIGHT else 1
        first, then = ((step - 1) * pw, step * pw) if d == RIGHT else (3 * pw, 2 * pw)
        src = tok.at[pl.ds(slot_at(sign * (step - 1)) * rows, rows), pl.ds(first, n)]
        dst = tok.at[pl.ds(slot_at(sign * step) * rows, rows), pl.ds(then, n)]
        at = (mb, d, step - 1)
        return remote(src, dst, z_send.at[at], z_recv.at[at], z_to[d])

    def shared_weight(f, which):
        e = (z + NZ + (1, 2, -4, -5)[f]) % NZ
        to = at_z((1, 2, -1, -2)[f])
        if which < 2:
            src = (wg_hbm, wu_hbm)[which].at[part_at(e), :]
            dst = wgu.at[pl.ds((4 + f) * pw, pw), pl.ds(which * bw, bw)]
        else:
            src = wd_hbm.at[:, part_at(e)]
            dst = wd.at[4 + f, pl.ds(0, bw), :]
        return remote(src, dst, w_send.at[f, which], w_recv.at[f, which], to)

    def weight_copy(d, piece):
        j = 2 if d == RIGHT else 1
        half = 2 * pw
        if piece < 2:
            at = pl.ds(piece * 4 * pw, 4 * pw)
            src = wgu.at[at, pl.ds(0, 2 * bw)]
            dst = wgu.at[at, pl.ds(j * 2 * bw, 2 * bw)]
        elif piece < 4:
            at = pl.ds((piece - 2) * 4 * pw + d * half, half)
            src = wgu.at[at, pl.ds(j * 2 * bw, 2 * bw)]
            dst = wgu.at[at, pl.ds(3 * 2 * bw, 2 * bw)]
        elif piece < 8:
            at = pl.ds((piece - 4) * qcols, qcols)
            src = wd.at[:, pl.ds(0, bw), at]
            dst = wd.at[:, pl.ds(j * bw, bw), at]
        else:
            at = pl.ds((piece - 8) * qcols, qcols)
            hb = bw // 2
            src = wd.at[:, pl.ds(j * bw + d * hb, hb), at]
            dst = wd.at[:, pl.ds(3 * bw + d * hb, hb), at]
        return remote(src, dst, y_send.at[d, piece], y_recv.at[d, piece], y_to[d])

    def saved_copy(peer, which):
        step = (1, -1, 2)[peer]
        src = (sg_hbm, su_hbm)[which].at[:, (y + NY + step) % NY]
        dst = (sg, su)[which].at[(2, 1, 3)[peer]]
        at = (peer, which)
        return remote(src, dst, s_send.at[at], s_recv.at[at], at_y(step))

    def to_owner(src, dst, kind, f):
        return remote(
            src.at[f], dst.at[f], x_send.at[kind, f], x_recv.at[kind, f], at_z(FOREIGN[f])
        )

    def to_helper(src, dst, kind, f):
        return remote(
            src, dst.at[f], x_send.at[kind, f], x_recv.at[kind, f], at_z(-FOREIGN[f])
        )

    def ring_copy(d, step, c):
        b = c % RING
        return remote(
            sbufs[step - 1].at[d, b],
            rbufs[step - 1].at[d, b],
            r_send.at[d, step - 1, b],
            r_recv.at[d, step - 1, b],
            z_to[d],
        )

    def out_copy(mb, c, i):
        e = part_of(i - 2)
        to = (p_next, k) if mb == 0 else (p_prev, k)
        return remote(
            obuf.at[c % RING, :, pl.ds(i * cols, cols)],
            (out_f, out_b)[mb].at[:, pl.ds(aligned(e * pw + c * cols, cols), cols)],
            o_send.at[c % RING, i],
            o_recv.at[mb, c, i],
            to,
        )

    own_rows = pl.ds(0, rows)
    pairs = []
    for i in range(NZ):
        pairs.append(
            (act_hbm.at[:, part_at(part_of(i - 2))], tok_f.at[own_rows, pl.ds(i * pw, pw)])
        )
    for p in range(4):
        e = part_at(part_of(p))
        pairs.append((wg_hbm.at[e, :], wgu.at[pl.ds(p * pw, pw), pl.ds(0, bw)]))
        pairs.append((wu_hbm.at[e, :], wgu.at[pl.ds(p * pw, pw), pl.ds(bw, bw)]))
    first_local = len(pairs)
    for i in range(NZ):
        e = part_at(part_of(i - 2))
        pairs.append((act_hbm.at[:, e], base_f.at[:, pl.ds(i * pw, pw)]))
        pairs.append((grad_hbm.at[:, e], tok_b.at[own_rows, pl.ds(i * pw, pw)]))
    for p in range(4):
        pairs.append((wd_hbm.at[:, part_at(part_of(p))], wd.at[p, pl.ds(0, bw), :]))
    pairs.append((sg_hbm.at[:, y], sg.at[0]))
    pairs.append((su_hbm.at[:, y], su.at[0]))
    local = [pltpu.make_async_copy(s, d, local_sem.at[i]) for i, (s, d) in enumerate(pairs)]

    for copy in local:
        copy.start()
    barrier = pltpu.get_barrier_semaphore()
    peers = [at_z(s) for s in (1, -1, 2, -2)] + [at_y(s) for s in (1, -1, 2)]
    peers += [(p_next, k), (p_prev, k)]
    for to in peers:
        pl.semaphore_signal(barrier, inc=1, device_id=to, device_id_type=MESH)
    pl.semaphore_wait(barrier, len(peers))

    for which in range(3):
        for f in (1, 3, 0, 2):
            shared_weight(f, which).start()
    for copy in local[:first_local]:
        copy.wait()
    for d in (0, 1):
        weight_copy(d, 0).start()
        token_copy(0, d, 1).start()

    def pass_tokens(mb, step):
        for d in (0, 1):
            token_copy(mb, d, step).wait_recv()
            if step < STEPS:
                token_copy(mb, d, step + 1).start()

    def pass_weights(piece, onward):
        for d in (0, 1):
            weight_copy(d, piece).wait_recv()
            weight_copy(d, onward).start()

    def turn(j):
        return (y + j + j // 2 - 2 * (j // 3)) % NY

    def mask_at(mask, zb, j, owner, b):
        return mask[zb * NY + turn(j), (owner * NY + y) * blocks + b].astype(F32)

    def source(i):
        return (z + NZ + Z_REL[i]) % NZ

    def packed_at(owner):
        return pl.ds(aligned(owner * BLOCK, BLOCK), BLOCK)

    def pack(mask, zb, j, lanes, put):
        for i in range(NZ):
            owner = source(i)
            total = None
            for b in range(blocks):
                piece = acc[pl.ds(i * rows + b * BLOCK, BLOCK), lanes]
                piece = piece * mask_at(mask, zb, j, owner, b)
                total = piece if total is None else total + piece
            put(owner, total)

    def unpack(mask, zb, packed, w, put):
        @pl.loop(0, NY)
        def _(j):
            lanes = pl.ds(aligned(j * w, w), w)
            for i in range(NZ):
                owner = source(i)
                value = packed[packed_at(owner), lanes].astype(F32)
                for b in range(blocks):
                    on = mask_at(mask, zb, j, owner, b)
                    put(pl.ds(i * rows + b * BLOCK, BLOCK), lanes, (value * on).astype(BF16))

    helped = [(z + NZ + s) % NZ for s in FOREIGN]
    both = pl.ds(0, 2 * bw)

    def gates_for(j_from, j_to):
        @pl.loop(j_from, j_to)
        def _(j):
            lanes = pl.ds(aligned(j * 2 * bw, 2 * bw), 2 * bw)
            acc[:, both] = jnp.zeros((NZ * rows, 2 * bw), F32)

            @pl.loop(0, 4)
            def _(p):
                acc[:, both] += jnp.dot(
                    tok_f[:, pl.ds(aligned((p + 2) * pw, pw), pw)],
                    wgu[pl.ds(aligned(p * pw, pw), pw), lanes],
                    preferred_element_type=F32,
                )

            def put_own(owner, value):
                pk_own[packed_at(owner), lanes] = value

            pack(mask_f, z, j, both, put_own)
            for f in range(4):
                acc[:, both] = jnp.dot(
                    tok_f[:, pl.ds((FOREIGN_PLACE[f] + 2) * pw, pw)],
                    wgu[pl.ds((4 + f) * pw, pw), lanes],
                    preferred_element_type=F32,
                )

                def put(owner, value):
                    pk_send[f, packed_at(owner), lanes] = value.astype(BF16)

                pack(mask_f, helped[f], j, both, put)

    for f in range(4):
        for which in (0, 1):
            shared_weight(f, which).wait_recv()
    for d in (0, 1):
        weight_copy(d, 1).start()
    pass_weights(0, 2)
    for step in (1, 2, 3):
        pass_tokens(0, step)
    pass_weights(1, 3)
    for copy in local[first_local:]:
        copy.wait()
    for f in range(4):
        shared_weight(f, 2).wait_recv()
    for d in (0, 1):
        weight_copy(d, 4).start()
    pass_tokens(0, 4)
    for d in (0, 1):
        token_copy(1, d, 1).start()
    pass_tokens(0, 5)
    gates_for(0, 3)
    pass_tokens(1, 1)
    pass_tokens(1, 2)
    for d in (0, 1):
        weight_copy(d, 2).wait_recv()
        weight_copy(d, 3).wait_recv()
    gates_for(3, 4)
    for f in range(4):
        to_owner(pk_send, pk_recv, 0, f).start()
    pass_tokens(1, 3)
    for f in range(4):
        to_owner(pk_send, pk_recv, 0, f).wait_recv()
    for j in range(NY):
        sums = []
        for lanes in (pl.ds(2 * j * bw, bw), pl.ds((2 * j + 1) * bw, bw)):
            total = pk_own[:, lanes]
            for f in range(4):
                total = total + pk_recv[f, :, lanes].astype(F32)
            sums.append(total)
        hidp[:, pl.ds(j * bw, bw)] = (jnp.maximum(sums[0], 0.0) * sums[1]).astype(BF16)
    for f in range(4):
        to_helper(hidp, hid_recv, 1, f).start()
    pass_weights(4, 8)
    for d in (0, 1):
        weight_copy(d, 5).start()
    pass_tokens(1, 4)

    def put_hidden(i):
        def put(at, lanes, value):
            hid[i, at, lanes] = value

        return put

    unpack(mask_f, z, hidp, bw, put_hidden(0))
    for f in range(4):
        to_helper(hidp, hid_recv, 1, f).wait_recv()
        unpack(mask_f, helped[f], hid_recv.at[f], bw, put_hidden(1 + f))
    ghp[...] = jnp.zeros(ghp.shape, F32)
    for d in (0, 1):
        for step in range(1, STEPS + 1):
            token_copy(0, d, step).wait_send()

    n_part = part.shape[0]

    def grad_hidden(q):
        lo = q * qcols
        at = pl.ds(aligned(lo, qcols), qcols)

        def add(i, zb):
            @pl.loop(0, NY)
            def _(j):
                lanes = pl.ds(aligned(j * bw, bw), bw)

                def put(owner, value):
                    ghp[i, packed_at(owner), lanes] += value

                pack(mask_b, zb, j, lanes, put)

        acc[...] = jnp.zeros(acc.shape, F32)

        @pl.loop(0, 4)
        def _(p):
            mine = pl.ds(aligned((p + 2) * pw + lo, qcols), qcols)
            acc[...] += dot_last(tok_b[:, mine], wd[p, :, at])

        add(0, z)
        for f in range(4):
            mine = pl.ds(aligned((FOREIGN_PLACE[f] + 2) * pw + lo, qcols), qcols)
            acc[...] = dot_last(tok_b[:, mine], wd[4 + f, :, at])
            add(1 + f, helped[f])

    def grads_packed():
        @pl.loop(0, NY)
        def _(j):
            lanes = pl.ds(aligned(j * bw, bw), bw)
            for owner in range(NZ):
                at = pl.ds(owner * BLOCK, BLOCK)
                grad = ghp[0, at, lanes]
                for f in range(4):
                    grad = grad + gh_recv[f, at, lanes].astype(F32)
                gate = up = None
                for b in range(blocks):
                    on = mask_at(mask_b, z, j, owner, b)
                    in_block = pl.ds(b * BLOCK, BLOCK)
                    g = sg[j, owner, in_block, :].astype(F32) * on
                    u = su[j, owner, in_block, :].astype(F32) * on
                    gate = g if gate is None else gate + g
                    up = u if up is None else up + u
                gradp[at, pl.ds(aligned(2 * j * bw, bw), bw)] = jnp.where(
                    gate > 0, grad * up, 0.0
                ).astype(BF16)
                gradp[at, pl.ds(aligned((2 * j + 1) * bw, bw), bw)] = (
                    grad * jnp.maximum(gate, 0.0)
                ).astype(BF16)

    def put_grads(i):
        def put(at, lanes, value):
            tok_f[at, pl.ds(i * 2 * NY * bw + lanes.start, 2 * bw)] = value

        return put

    def side_work(t):
        for q in range(1, QUARTERS):

            @pl.when(t == 2 * q - 1)
            def _():
                pass_weights(4 + q, 8 + q)
                if q < QUARTERS - 1:
                    for d in (0, 1):
                        weight_copy(d, 5 + q).start()
                else:
                    for peer in range(3):
                        for which in (0, 1):
                            saved_copy(peer, which).start()

        for q in range(QUARTERS):

            @pl.when(t == 2 * q)
            def _():
                for d in (0, 1):
                    weight_copy(d, 8 + q).wait_recv()

        @pl.when(t == 3)
        def _():
            pass_tokens(1, 5)

        @pl.when((t >= 3) & (t < 7))
        def _():
            grad_hidden(t - 3)

        @pl.when(t == 6)
        def _():
            for f in range(4):
                gh_send[f] = ghp[1 + f].astype(BF16)
                to_owner(gh_send, gh_recv, 2, f).start()

        @pl.when(t == 7)
        def _():
            for peer in range(3):
                for which in (0, 1):
                    saved_copy(peer, which).wait_recv()
            for f in range(4):
                to_owner(gh_send, gh_recv, 2, f).wait_recv()
            grads_packed()
            for f in range(4):
                to_helper(gradp, grad_recv, 3, f).start()

        @pl.when(t == 8)
        def _():
            unpack(mask_b, z, gradp, 2 * bw, put_grads(0))
            for f in range(4):
                to_helper(gradp, grad_recv, 3, f).wait_recv()
                unpack(mask_b, helped[f], grad_recv.at[f], 2 * bw, put_grads(1 + f))

    def local_part(t):
        def put(p, value):
            part[t % n_part, :, pl.ds(p * cols, cols)] = value

        @pl.when(t < chunks)
        def _():
            at = pl.ds(aligned(t * cols, cols), cols)
            for p in range(4):
                total = jnp.dot(hid[0], wd[p, :, at], preferred_element_type=F32)
                for f in range(4):
                    if FOREIGN_PLACE[f] == p:
                        total = total + jnp.dot(
                            hid[1 + f], wd[4 + f, :, at], preferred_element_type=F32
                        )
                put(p, total)

        @pl.when((t >= chunks) & (t < 2 * chunks))
        def _():
            def grads(i):
                return tok_f[:, pl.ds(i * 2 * NY * bw, 2 * NY * bw)]

            def weights(i):
                return wgu[pl.ds(aligned(i * pw + (t - chunks) * cols, cols), cols), :]

            for p in range(4):
                total = dot_last(grads(0), weights(p))
                for f in range(4):
                    if FOREIGN_PLACE[f] == p:
                        total = total + dot_last(grads(1 + f), weights(4 + f))
                put(p, total)

    def ring_step(step, c):
        b = c % RING
        pb = c % n_part
        for d in (0, 1):
            if step > 1:
                ring_copy(d, step - 1, c).wait_recv()

            @pl.when(c >= RING)
            def _():
                ring_copy(d, step, c - RING).wait_send()

            ahead = (STEPS + 1 - step) * (1 if d == RIGHT else -1)
            at = pl.ds(slot_at(ahead) * rows, rows)
            s = sbufs[step - 1]
            r = rbufs[step - 2]

            def mine(first, n):
                return part[pb, at, pl.ds(first * cols, n * cols)]

            def came(first, n):
                return r[d, b, :, pl.ds(first * cols, n * cols)]

            def put(first, n, value):
                s[d, b, :, pl.ds(first * cols, n * cols)] = value.astype(BF16)

            if d == RIGHT:
                put(0, 1, mine(0, 1))
                n = min(step, 4) - 1
                if n:
                    put(1, n, mine(1, n) + came(0, n).astype(F32))
                if step == STEPS:
                    put(4, 1, came(3, 1))
            else:
                put(step - 1, 1, mine(3, 1))
                skip = 1 if step == STEPS else 0
                n = step - 1 - skip
                if n:
                    put(skip, n, mine(3 - n, n) + came(skip, n).astype(F32))
                if skip:
                    put(0, 1, came(0, 1))
            ring_copy(d, step, c).start()

    def finish(c):
        b = c % RING
        for d in (0, 1):
            ring_copy(d, STEPS, c).wait_recv()

        @pl.when(c >= RING)
        def _():
            for i in range(NZ):
                out_copy(0, (c - RING) % chunks, i).wait_send()

        for mb in (0, 1):

            @pl.when((c >= mb * chunks) & (c < (mb + 1) * chunks))
            def _():
                cc = c - mb * chunks
                base = base_f if mb == 0 else tok_b
                for i in range(NZ):
                    at = pl.ds(aligned(i * pw + cc * cols, cols), cols)
                    total = base[own_rows, at].astype(F32)
                    if i < 5:
                        total += rbufs[4][LEFT, b, :, pl.ds(i * cols, cols)].astype(F32)
                    if i > 2:
                        total += rbufs[4][RIGHT, b, :, pl.ds((i - 3) * cols, cols)].astype(F32)
                    if 2 <= i < 6:
                        total += part[c % n_part, own_rows, pl.ds((i - 2) * cols, cols)]
                    obuf[b, :, pl.ds(i * cols, cols)] = total.astype(BF16)
                    out_copy(mb, cc, i).start()

    total = 2 * chunks

    @pl.loop(0, total + STEPS)
    def _(t):
        side_work(t)
        local_part(t)
        for step in range(1, STEPS + 1):

            @pl.when((t >= step - 1) & (t < total + step - 1))
            def _():
                ring_step(step, t - (step - 1))

        @pl.when(t >= STEPS)
        def _():
            finish(t - STEPS)

    @pl.loop(total - RING, total)
    def _(c):
        for d in (0, 1):
            for step in range(1, STEPS + 1):
                ring_copy(d, step, c).wait_send()
        for i in range(NZ):
            out_copy(1, c - chunks, i).wait_send()

    for d in (0, 1):
        for step in range(1, STEPS + 1):
            token_copy(1, d, step).wait_send()
        for piece in range(12):
            weight_copy(d, piece).wait_send()
    for f in range(4):
        for which in range(3):
            shared_weight(f, which).wait_send()
        to_owner(pk_send, pk_recv, 0, f).wait_send()
        to_helper(hidp, hid_recv, 1, f).wait_send()
        to_owner(gh_send, gh_recv, 2, f).wait_send()
        to_helper(gradp, grad_recv, 3, f).wait_send()
    for peer in range(3):
        for which in (0, 1):
            saved_copy(peer, which).wait_send()

    @pl.loop(0, chunks)
    def _(c):
        for mb in (0, 1):
            for i in range(NZ):
                out_copy(mb, c, i).wait_recv()


def per_device(act_fwd, grad_in, w_gate, w_up, w_down, saved_gate, saved_up, mask_fwd, mask_bwd):
    rows, width = act_fwd.shape[1:]
    bw = w_gate.shape[2]
    chunks = 8
    pw = width // NZ
    cols = pw // chunks
    all_rows = NZ * rows
    packed = NZ * BLOCK
    by_owner = (NZ, NY, rows, bw)
    anywhere = pl.BlockSpec(memory_space=pl.ANY)
    scalars = pl.BlockSpec(memory_space=pltpu.SMEM)
    dma = pltpu.SemaphoreType.DMA
    out = jax.ShapeDtypeStruct((rows, width), BF16)
    ring = [pltpu.VMEM((2, RING, rows, n * cols), BF16) for n in range(1, STEPS + 1)]
    ahead, behind = pl.pallas_call(
        functools.partial(kernel, chunks),
        out_shape=(out, out),
        in_specs=[anywhere] * 7 + [scalars] * 2,
        out_specs=(anywhere, anywhere),
        scratch_shapes=[
            pltpu.VMEM((all_rows, width), BF16),
            pltpu.VMEM((all_rows, width), BF16),
            pltpu.VMEM((width, NY * 2 * bw), BF16),
            pltpu.VMEM((NZ, NY * bw, pw), BF16),
            pltpu.VMEM((NY, NZ, rows, bw), BF16),
            pltpu.VMEM((NY, NZ, rows, bw), BF16),
            pltpu.VMEM((5, all_rows, NY * bw), BF16),
            pltpu.VMEM((all_rows, NY * bw), F32),
            pltpu.VMEM((rows, width), BF16),
            pltpu.VMEM((packed, NY * 2 * bw), F32),
            pltpu.VMEM((4, packed, NY * 2 * bw), BF16),
            pltpu.VMEM((4, packed, NY * 2 * bw), BF16),
            pltpu.VMEM((packed, NY * bw), BF16),
            pltpu.VMEM((4, packed, NY * bw), BF16),
            pltpu.VMEM((5, packed, NY * bw), F32),
            pltpu.VMEM((4, packed, NY * bw), BF16),
            pltpu.VMEM((4, packed, NY * bw), BF16),
            pltpu.VMEM((packed, NY * 2 * bw), BF16),
            pltpu.VMEM((4, packed, NY * 2 * bw), BF16),
            pltpu.VMEM((STEPS + 1, all_rows, 4 * cols), F32),
            pltpu.VMEM((RING, rows, NZ * cols), BF16),
            *ring,
            *ring,
            dma((38,)),
            dma((2, 2, STEPS)),
            dma((2, 2, STEPS)),
            dma((4, 3)),
            dma((4, 3)),
            dma((2, 12)),
            dma((2, 12)),
            dma((3, 2)),
            dma((3, 2)),
            dma((4, 4)),
            dma((4, 4)),
            dma((2, STEPS, RING)),
            dma((2, STEPS, RING)),
            dma((RING, NZ)),
            dma((2, chunks, NZ)),
        ],
        compiler_params=pltpu.CompilerParams(
            collective_id=0, has_side_effects=True, vmem_limit_bytes=67043328
        ),
    )(
        act_fwd[0],
        grad_in[0],
        w_gate[0],
        w_up[0],
        w_down[0],
        saved_gate[0].reshape(by_owner),
        saved_up[0].reshape(by_owner),
        mask_fwd[0].T,
        mask_bwd[0].T,
    )
    return ahead[None], behind[None]


def solution(mesh):
    in_specs = (
        P("pipe", "bundle", None),
        P("pipe", "bundle", None),
        P("pipe", None, "bundle"),
        P("pipe", None, "bundle"),
        P("pipe", "bundle", None),
        P("pipe", None, "bundle"),
        P("pipe", None, "bundle"),
        P("pipe", None, None),
        P("pipe", None, None),
    )
    out_specs = (P("pipe", "bundle", None), P("pipe", "bundle", None))
    return jax.shard_map(
        per_device, mesh=mesh, in_specs=in_specs, out_specs=out_specs, check_vma=False
    )
```

time: 854 us -> 338 us (0.40)
  blocking collectives: 376 us -> 0 us
  waiting for transfers between devices: 347 us -> 0 us
  Pallas kernels: 0 us -> 334 us
  matrix products: 69.9 us -> 0 us
  local copies, waits for them, and re-layouts: 32.4 us -> 3.32 us
  starting transfers between devices: 17.5 us -> 0 us
    all_to_all x1 -> x0, blocking collectives: 376 us -> none  [side_by_side(): lax.all_to_all(both, axis, split_axis=split_dim, concat_axis=concat_dim,...]
    pallas_call x0 -> x1, Pallas kernels: none -> 334 us  [per_device(): pl.pallas_call(functools.partial(kernel, chunks), out_shape=(out, out), i...]
    all_to_all x2 -> x0, waiting for transfers between devices: 333 us -> none  [the longest x1 173 us: per_device(): lax.all_to_all(parts_b, 'bundle', split_axis=0, concat_axis=0, tiled=True)]
    dot_general x12 -> x0, matrix products: 69.9 us -> none  [the longest x3 25.2 us: contract_last(): lax.dot_general(left, right, (((1,), (1,)), ((), ())), preferred_element_...]
    concatenate x1 -> x0, local copies, waits for them, and re-layouts: 22.2 us -> none  [side_by_side(): both = jnp.concatenate(arrays, axis=along)]
    ppermute x2 -> x0, waiting for transfers between devices: 13.6 us -> none  [shifted(): return lax.ppermute(value, axis, pairs)]
    all_to_all x2 -> x0, starting transfers between devices: 13.2 us -> none  [the longest x1 7.03 us: per_device(): lax.all_to_all(parts_f, 'bundle', split_axis=0, concat_axis=0, tiled=True)]
  transfers between devices with their start and end apart: 4 -> 0, of which waited for: 3 -> 0; matrix products, arithmetic and copies ran while one was open for 7% -> 0% of each run, Pallas kernels for 0% -> 0%
where the time goes in v3:
time: 338 us
  Pallas kernels  334 us (99%)
    pallas_call x1, Pallas kernels, per_device(): pl.pallas_call(functools.partial(kernel, chunks), out_shape=(out, out), i...  334 us

profile of v3, /device:TPU:1, one launch (start us, length us, event | category | flops | bytes accessed | tf_op | source)
XLA Modules:
  0.0 337.9 jit_solution(4458010108538767824)
XLA Ops:
  0.6 333.9 %shard_map.104 = (bf16[64,8192]{1,0:T(8,128)(2,1)}, bf16[64,8192]{1,0:T(8,128)(2,1)}) custom-call(bf16[64,8192]{1,0:T(8,128)(2,1)} %bitcast.18, bf16[64,8192]{1,0:T(8,128)(2,1)} %bitcast.19, bf16[8192,128]{1,0:T(8,128)(2,1)} %bitcast.15, bf16[8192,128]{1,0:T(8,128)(2,1)} %bitcast.16, bf16[128,8192]{1,0:T(8,128)(2,1)} %bitcast.17, ...), custom_call_target="tpu_custom_call" | custom-call | tf_op jit(solution)/shard_map/pallas_call | solution.py:618
  334.6 0.0 copy-start
  334.6 2.4 copy.13
  336.9 0.0 copy-done
  336.9 1.0 copy.14
Async XLA Ops:
  334.6 2.4 copy-start

commit v4 on v3

--- a/solution.py
+++ b/solution.py
@@ -18,6 +18,7 @@
 STEPS = 5
 FOREIGN = (-1, -2, 1, 2)
 FOREIGN_PLACE = (0, 0, 3, 3)
+AWAY = (-1, -1, 1, 1)
 
 
 def slot_at(rel):
@@ -135,13 +136,33 @@
 
     def to_owner(src, dst, kind, f):
         return remote(
-            src.at[f], dst.at[f], x_send.at[kind, f], x_recv.at[kind, f], at_z(FOREIGN[f])
+            src.at[f], dst.at[f], x_send.at[kind, f], x_recv.at[kind, f], at_z(AWAY[f])
         )
 
     def to_helper(src, dst, kind, f):
+        src = dst.at[f - 1] if f % 2 else src
         return remote(
-            src, dst.at[f], x_send.at[kind, f], x_recv.at[kind, f], at_z(-FOREIGN[f])
+            src, dst.at[f], x_send.at[kind, f], x_recv.at[kind, f], at_z(-AWAY[f])
         )
+
+    def start_owner(src, dst, kind):
+        for f in (1, 3):
+            to_owner(src, dst, kind, f).start()
+
+    def join_owner(src, dst, kind):
+        for f in (1, 3):
+            to_owner(src, dst, kind, f).wait_recv()
+            src[f - 1] = (src[f - 1].astype(F32) + dst[f].astype(F32)).astype(BF16)
+            to_owner(src, dst, kind, f - 1).start()
+
+    def start_helpers(src, dst, kind):
+        for f in (0, 2):
+            to_helper(src, dst, kind, f).start()
+
+    def pass_helpers(src, dst, kind):
+        for f in (0, 2):
+            to_helper(src, dst, kind, f).wait_recv()
+            to_helper(src, dst, kind, f + 1).start()
 
     def ring_copy(d, step, c):
         b = c % RING
@@ -306,24 +327,23 @@
         weight_copy(d, 2).wait_recv()
         weight_copy(d, 3).wait_recv()
     gates_for(3, 4)
-    for f in range(4):
-        to_owner(pk_send, pk_recv, 0, f).start()
+    start_owner(pk_send, pk_recv, 0)
     pass_tokens(1, 3)
-    for f in range(4):
+    join_owner(pk_send, pk_recv, 0)
+    pass_weights(4, 8)
+    for d in (0, 1):
+        weight_copy(d, 5).start()
+    for f in (0, 2):
         to_owner(pk_send, pk_recv, 0, f).wait_recv()
     for j in range(NY):
         sums = []
         for lanes in (pl.ds(2 * j * bw, bw), pl.ds((2 * j + 1) * bw, bw)):
             total = pk_own[:, lanes]
-            for f in range(4):
+            for f in (0, 2):
                 total = total + pk_recv[f, :, lanes].astype(F32)
             sums.append(total)
         hidp[:, pl.ds(j * bw, bw)] = (jnp.maximum(sums[0], 0.0) * sums[1]).astype(BF16)
-    for f in range(4):
-        to_helper(hidp, hid_recv, 1, f).start()
-    pass_weights(4, 8)
-    for d in (0, 1):
-        weight_copy(d, 5).start()
+    start_helpers(hidp, hid_recv, 1)
     pass_tokens(1, 4)
 
     def put_hidden(i):
@@ -333,8 +353,10 @@
         return put
 
     unpack(mask_f, z, hidp, bw, put_hidden(0))
-    for f in range(4):
-        to_helper(hidp, hid_recv, 1, f).wait_recv()
+    pass_helpers(hidp, hid_recv, 1)
+    for f in (0, 2, 1, 3):
+        if f % 2:
+            to_helper(hidp, hid_recv, 1, f).wait_recv()
         unpack(mask_f, helped[f], hid_recv.at[f], bw, put_hidden(1 + f))
     ghp[...] = jnp.zeros(ghp.shape, F32)
     for d in (0, 1):
@@ -377,7 +399,7 @@
             for owner in range(NZ):
                 at = pl.ds(owner * BLOCK, BLOCK)
                 grad = ghp[0, at, lanes]
-                for f in range(4):
+                for f in (0, 2):
                     grad = grad + gh_recv[f, at, lanes].astype(F32)
                 gate = up = None
                 for b in range(blocks):
@@ -433,24 +455,24 @@
         def _():
             for f in range(4):
                 gh_send[f] = ghp[1 + f].astype(BF16)
-                to_owner(gh_send, gh_recv, 2, f).start()
+            start_owner(gh_send, gh_recv, 2)
 
         @pl.when(t == 7)
         def _():
             for peer in range(3):
                 for which in (0, 1):
                     saved_copy(peer, which).wait_recv()
-            for f in range(4):
+            for f in (0, 2):
                 to_owner(gh_send, gh_recv, 2, f).wait_recv()
             grads_packed()
-            for f in range(4):
-                to_helper(gradp, grad_recv, 3, f).start()
+            start_helpers(gradp, grad_recv, 3)
 
         @pl.when(t == 8)
         def _():
             unpack(mask_b, z, gradp, 2 * bw, put_grads(0))
-            for f in range(4):
-                to_helper(gradp, grad_recv, 3, f).wait_recv()
+            for f in (0, 2, 1, 3):
+                if f % 2:
+                    to_helper(gradp, grad_recv, 3, f).wait_recv()
                 unpack(mask_b, helped[f], grad_recv.at[f], 2 * bw, put_grads(1 + f))
 
     def local_part(t):
@@ -569,6 +591,14 @@
         @pl.when(t >= STEPS)
         def _():
             finish(t - STEPS)
+
+        @pl.when(t == chunks - 2)
+        def _():
+            join_owner(gh_send, gh_recv, 2)
+
+        @pl.when(t == chunks - 1)
+        def _():
+            pass_helpers(gradp, grad_recv, 3)
 
     @pl.loop(total - RING, total)
     def _(c):

time: 338 us -> 328 us (0.970)
  Pallas kernels: 334 us -> 323 us
    pallas_call x1, Pallas kernels: 334 us -> 323 us  [per_device(): pl.pallas_call(functools.partial(kernel, chunks), out_shape=(out, out), i...]
where the time goes in v4:
time: 328 us; the launch traced here: 327 us
  Pallas kernels  323 us (98%)
  local copies, waits for them, and re-layouts  3.32 us (1%)
    pallas_call x1, Pallas kernels, per_device(): pl.pallas_call(functools.partial(kernel, chunks), out_shape=(out, out), i...  323 us

profile of v4, /device:TPU:1, one launch (start us, length us, event | category | flops | bytes accessed | tf_op | source)
XLA Modules:
  0.0 327.3 jit_solution(3055918610233066087)
XLA Ops:
  0.6 323.4 %shard_map.104 = (bf16[64,8192]{1,0:T(8,128)(2,1)}, bf16[64,8192]{1,0:T(8,128)(2,1)}) custom-call(bf16[64,8192]{1,0:T(8,128)(2,1)} %bitcast.18, bf16[64,8192]{1,0:T(8,128)(2,1)} %bitcast.19, bf16[8192,128]{1,0:T(8,128)(2,1)} %bitcast.15, bf16[8192,128]{1,0:T(8,128)(2,1)} %bitcast.16, bf16[128,8192]{1,0:T(8,128)(2,1)} %bitcast.17, ...), custom_call_target="tpu_custom_call" | custom-call | tf_op jit(solution)/shard_map/pallas_call | solution.py:648
  324.0 0.0 copy-start
  324.0 2.4 copy.13
  326.4 0.0 copy-done
  326.4 1.0 copy.14
Async XLA Ops:
  324.0 2.4 copy-start
